TPU v7x, 256 devices: a whole 4x4x8 slice. The times are simulated.
256 devices in a mesh: grp: 8 (over y_hi, x), aux: 32 (over y_lo, z, core).
Axes of the slice: x: 4, y: 4 (y_hi: 2, y_lo: 2; y = y_hi * 2 + y_lo), z: 8, core: 2. Of those that a mesh axis runs over, the one named last changes fastest.
Arguments:
- integrals: bfloat16 [2048, 256, 512], P('aux', 'grp'), may hold values from -0.75 to 0.75
- metric: bfloat16 [2048, 2048], replicated, may hold values from -0.125 to 0.125
- occupied_energy: float32 [256], replicated, may hold values from -2 to -0.5
- virtual_energy: float32 [512], replicated, may hold values from 0.2 to 3
- plan: int32 [4, 32], replicated, may hold values from 0 to 7
Outputs:
- density: bfloat16 [2048, 256, 512], P('aux', 'grp')
All inputs are finite; a program needn't handle non-finite values.
Results may differ from a plain program's by a relative error of at most 0.0053.
Values may be sent and summed in bfloat16 or wider, within the bound.
No kernel may reach another device: no remote copies, remote signals or barrier semaphores. Data moves between devices by JAX's collectives and lax.ppermute only.
A program may use at most 128 MiB of HBM per device.

v0:
```python
import jax
import jax.numpy as jnp
from jax import lax
from jax.sharding import Mesh
from jax.sharding import PartitionSpec as P

AUX = ("aux_0", "aux_1", "aux_2")


def broadcast(array, axis, root):
    return lax.dynamic_index_in_dim(lax.all_gather(array, axis), root, 0, keepdims=False)


def cut_along(array, dim, count):
    dims = array.shape
    pieces = array.reshape(*dims[:dim], count, dims[dim] // count, *dims[dim + 1 :])
    return jnp.moveaxis(pieces, dim, 0)


def in_order(pieces, dim):
    pieces = jnp.moveaxis(pieces, 0, dim)
    dims = pieces.shape
    return pieces.reshape(*dims[:dim], dims[dim] * dims[dim + 1], *dims[dim + 2 :])


def turned_blocks(pieces, axes, order):
    inside = pieces.shape[1:]
    filled = pieces.reshape(*(lax.axis_size(a) for a in axes), *inside)
    for k in order:
        filled = lax.all_to_all(filled, axes[k], k, k, tiled=True)
    return filled.reshape(-1, *inside)


def two_step_exchange(array, groups, order, split_dim, concat_dim):
    count = lax.axis_size(groups[0]) * lax.axis_size(groups[1])
    pieces = cut_along(array, split_dim, count)
    return in_order(turned_blocks(pieces, groups, order), concat_dim)


def pair_term(own_block, partner, own_energy, partner_energy, virtual_energy):
    coulomb = jnp.einsum("qia,qjb->ijab", own_block, partner, preferred_element_type=jnp.float32)
    denominator = (
        own_energy[:, None, None, None]
        + partner_energy[None, :, None, None]
        - virtual_energy[None, None, :, None]
        - virtual_energy[None, None, None, :]
    )
    amplitude = ((2.0 * coulomb - jnp.swapaxes(coulomb, 2, 3)) / denominator).astype(jnp.bfloat16)
    return jnp.einsum("ijab,qjb->qia", amplitude, partner, preferred_element_type=jnp.float32)


def body(integrals, metric, occupied_energy, virtual_energy, plan):
    shards = lax.axis_size(AUX)
    per_device = integrals.shape[1] // shards
    aux_rows = metric.shape[0]
    aux_place = lax.axis_index(AUX)
    block_index = lax.axis_index("grp") * shards + aux_place
    received = lax.all_to_all(integrals, AUX, split_axis=1, concat_axis=0, tiled=True)
    flattened = received.reshape(aux_rows, per_device * received.shape[2])
    own_block = jnp.dot(metric, flattened, preferred_element_type=jnp.float32)
    own_block = own_block.astype(jnp.bfloat16).reshape(received.shape)
    own_energy = lax.dynamic_slice_in_dim(occupied_energy, block_index * per_device, per_device)
    density_sum = jnp.zeros(own_block.shape, jnp.float32)
    for step_index in range(plan.shape[0]):
        owner_group = lax.dynamic_index_in_dim(plan[step_index], aux_place, 0, keepdims=False)
        partner = broadcast(own_block, "grp", owner_group)
        first_index = (owner_group * shards + aux_place) * per_device
        partner_energy = lax.dynamic_slice_in_dim(occupied_energy, first_index, per_device)
        density_sum = density_sum + pair_term(
            own_block, partner, own_energy, partner_energy, virtual_energy
        )
    density = density_sum.astype(jnp.bfloat16)
    return two_step_exchange(density, (("aux_0", "aux_1"), "aux_2"), (1, 0), 0, 1)


def solution(mesh):
    split = Mesh(
        mesh.devices.reshape(mesh.shape["grp"], 2, 8, 2), ("grp", "aux_0", "aux_1", "aux_2")
    )
    placed = (P(AUX, "grp", None), P(), P(), P(), P())
    return jax.shard_map(
        body, mesh=split, in_specs=placed, out_specs=P(AUX, "grp", None), check_vma=False
    )
```

profile of v0, /device:TPU:32, one launch (start us, length us, event | category | flops | bytes accessed | tf_op | source)
XLA Modules:
  0.0 369.3 jit_solution(16133566435381391431)
XLA Ops:
  6.5 0.0 all-gather.3.cloned.1.call-start
  6.5 0.0 copy-start.10
  6.5 2.9 copy.23
  9.4 61.1 %all_to_all.25 = bf16[64,32,512]{2,0,1:T(8,128)(2,1)S(1)} all-to-all(bf16[64,32,512]{2,0,1:T(8,128)(2,1)S(1)} %copy.23), channel_id=1, replica_groups=mesh['grp'=8,'aux_0'=2,'aux_1'=8,'aux_2'=2] {'aux_0','aux_1','aux_2'}, dimensions={1} | all-to-all | bytes 4194304 | tf_op jit(solution)/shard_map/all_to_all | solution.py:58
  70.6 0.0 copy-done.10
  70.6 5.7 %convolution_convert_fusion = bf16[2048,512]{1,0:T(8,128)(2,1)} fusion(bf16[2048,2048]{1,0:T(8,128)(2,1)S(1)} %copy-done.10, bf16[2048,512]{1,0:T(8,128)(2,1)S(1)} %bitcast.129), kind=kOutput, calls=%fused_computation.1 | convolution fusion | flops 4296015872 | bytes 12582912 | tf_op jit(solution)/shard_map/dot_general | solution.py:60
  76.2 0.0 copy-start.9
  76.2 0.0 copy-start.8
  76.2 0.0 copy-start.7
  76.2 0.0 copy-start
  76.2 0.0 all-gather.3.cloned.1.call-update
  76.3 0.6 copy-done.9
  76.9 0.6 constant_dynamic-slice_fusion
  80.8 0.7 constant_dynamic-slice_fusion.2
  85.5 0.0 copy-done.8
  85.5 0.7 fusion.58
  93.9 0.0 copy-done.7
  93.9 170.1 %all-gather.3.cloned.1.call-done = bf16[16384,512]{1,0:T(8,128)(2,1)} async-done(((bf16[2048,512]{1,0:T(8,128)(2,1)}), bf16[16384,512]{1,0:T(8,128)(2,1)}) %all-gather.3.cloned.1.call-update) | async-done | bytes 16777232 | tf_op jit(solution)/shard_map/all_gather | solution.py:11
  264.0 0.0 copy-done
  264.0 2.9 fusion.1
  266.9 3.8 %fusion.5 = f32[512,512]{1,0:T(8,128)} fusion(bf16[2048,512]{1,0:T(8,128)(2,1)S(1)} %copy-done, bf16[8,2048,1,512]{3,1,0,2:T(8,128)(2,1)} %bitcast.131, s32[]{:T(128)S(6)} %select_n.41), kind=kOutput, calls=%fused_computation.7 | convolution fusion | flops 1073741824 | bytes 5242884 | tf_op jit(solution)/shard_map/qia,qjb->ijab/dot_general | solution.py:41
  270.7 3.8 %fusion.9 = f32[512,512]{1,0:T(8,128)} fusion(bf16[2048,512]{1,0:T(8,128)(2,1)S(1)} %copy-done, bf16[8,2048,1,512]{3,1,0,2:T(8,128)(2,1)} %bitcast.132, s32[]{:T(128)S(6)} %select_n.39), kind=kOutput, calls=%fused_computation.11 | convolution fusion | flops 1073741824 | bytes 5242884 | tf_op jit(solution)/shard_map/qia,qjb->ijab/dot_general | solution.py:41
  274.5 3.8 %fusion.13 = f32[512,512]{1,0:T(8,128)} fusion(bf16[2048,512]{1,0:T(8,128)(2,1)S(1)} %copy-done, bf16[8,2048,1,512]{3,1,0,2:T(8,128)(2,1)} %bitcast.133, s32[]{:T(128)S(6)} %select_n.36), kind=kOutput, calls=%fused_computation.15 | convolution fusion | flops 1073741824 | bytes 5242884 | tf_op jit(solution)/shard_map/qia,qjb->ijab/dot_general | solution.py:41
  278.4 0.0 copy-start.3
  278.4 0.0 copy-start.6
  278.4 2.7 copy.24
  281.1 0.0 copy-done.3
  281.1 1.3 copy.26
  282.4 0.0 copy-done.6
  282.4 1.3 copy.28
  283.7 0.3 copy.30
  284.1 0.0 copy-start.4
  284.1 0.0 copy-start.5
  284.1 3.5 fusion.3
  287.6 0.0 copy-done.4
  287.6 0.0 copy-done.5
  287.6 0.0 copy-start.1
  287.6 0.0 copy-start.2
  287.6 3.3 fusion.7
  290.9 0.0 copy-done.1
  290.9 0.0 copy-done.2
  290.9 3.1 fusion.11
  294.0 3.5 add_convert_fusion
  297.5 0.1 copy.31
  297.7 5.4 %all_to_all.26 = bf16[16,2,64,1,512]{4,2,0,3,1:T(8,128)(2,1)S(1)} all-to-all(bf16[16,2,64,1,512]{4,2,0,3,1:T(8,128)(2,1)S(1)} %copy.31), channel_id=1, replica_groups=mesh['grp'=8,'aux_0'=2,'aux_1'=8,'aux_2'=2] {'aux_2'}, dimensions={1} | all-to-all | bytes 4194304 | tf_op jit(solution)/shard_map/all_to_all | solution.py:30
  303.1 0.2 copy.32
  303.3 56.7 %all_to_all.27 = bf16[16,2,64,1,512]{4,2,1,3,0:T(8,128)(2,1)S(1)} all-to-all(bf16[16,2,64,1,512]{4,2,1,3,0:T(8,128)(2,1)S(1)} %copy.32), channel_id=1, replica_groups=mesh['grp'=8,'aux_0'=2,'aux_1'=8,'aux_2'=2] {'aux_0','aux_1'}, dimensions={0} | all-to-all | bytes 4194304 | tf_op jit(solution)/shard_map/all_to_all | solution.py:30
  360.0 2.5 copy.35
  (2 shorter events, 0.0 us)
Async XLA Ops:
  6.5 257.5 %all-gather.3.cloned.1.call-start = ((), (), s32[]{:S(2)}) async-start(), calls=%async_computation.3 | async-start | bytes 18874368 | tf_op jit(solution)/shard_map/all_gather | solution.py:11
  6.5 64.0 %copy-start.10 = (bf16[2048,2048]{1,0:T(8,128)(2,1)S(1)}, bf16[2048,2048]{1,0:T(8,128)(2,1)}, u32[]{:S(2)}) copy-start(bf16[2048,2048]{1,0:T(8,128)(2,1)} %param.6) | copy-start | bytes 25165828
  76.2 0.7 copy-start.9
  76.2 9.2 %copy-start.8 = (f32[256]{0:T(256)S(1)}, f32[256]{0:T(256)}, u32[]{:S(2)}) copy-start(f32[256]{0:T(256)} %param.7) | copy-start | bytes 3076
  76.2 17.7 %copy-start.7 = (f32[512]{0:T(512)S(1)}, f32[512]{0:T(512)}, u32[]{:S(2)}) copy-start(f32[512]{0:T(512)} %param.8) | copy-start | bytes 6148
  76.2 187.8 %copy-start = (bf16[2048,512]{1,0:T(8,128)(2,1)S(1)}, bf16[2048,512]{1,0:T(8,128)(2,1)}, u32[]{:S(2)}) copy-start(bf16[2048,512]{1,0:T(8,128)(2,1)} %convolution_convert_fusion) | copy-start | bytes 6291460
  278.4 2.7 copy-start.3
  278.4 4.1 %copy-start.6 = (f32[512,512]{1,0:T(8,128)S(1)}, f32[512,512]{1,0:T(8,128)}, u32[]{:S(2)}) copy-start(f32[512,512]{1,0:T(8,128)} %fusion.5) | copy-start | bytes 3145732
  284.1 3.5 copy-start.4
  284.1 3.5 copy-start.5
  287.6 3.3 copy-start.1
  287.6 3.3 copy-start.2
Sparse Core Ops, SparseCore 0:
  76.4 187.5 all-gather.2
where the time goes:
time: 370 us; the launch traced here: 369 us
  waiting for transfers between devices  170 us (46%)
  blocking collectives  123 us (33%)
  matrix products  33.4 us (9%)
  between operations  28.6 us (8%)
  local copies, waits for them, and re-layouts  14 us (4%)
    all_gather x1, waiting for transfers between devices, broadcast(): lax.all_gather(array, axis)  170 us
    all_to_all x2, blocking collectives, turned_blocks(): filled = lax.all_to_all(filled, axes[k], k, k, tiled=True)  62.1 us
    all_to_all x1, blocking collectives, body(): lax.all_to_all(integrals, AUX, split_axis=1, concat_axis=0, tiled=True)  61.1 us
    dot_general x4, matrix products, pair_term(): jnp.einsum('qia,qjb->ijab', own_block, partner, preferred_element_type=jn...  14.4 us
    dot_general x4, matrix products, pair_term(): jnp.einsum('ijab,qjb->qia', amplitude, partner, preferred_element_type=jn...  13.4 us
  transfers between devices with their start and end apart: 1, of which 1 were waited for; matrix products, arithmetic and copies ran while one was open for 1% of the time, Pallas kernels for 0%

commit v1 on v0

v1 whole, which is shorter than its diff:
```python
import jax
import jax.numpy as jnp
from jax import lax
from jax.experimental import pallas as pl
from jax.experimental.pallas import tpu as pltpu
from jax.sharding import Mesh
from jax.sharding import PartitionSpec as P

SPLIT = (("yh", 2), ("x", 4), ("yl", 2), ("z", 8), ("c", 2))
AUX = ("yl", "z", "c")
PLACE = ("c", "x")
CHUNKS = 2


def pair_kernel(energy_ref, own0, own1, part0, part1, row_ref, col_ref, out_ref, own_t, total):
    s = pl.program_id(0)
    half = own0.shape[1]

    @pl.when(s == 0)
    def _():
        own_t[:half, :] = own0[...].T
        own_t[half:, :] = own1[...].T

    partner = jnp.concatenate(
        [part0[...].reshape(own0.shape), part1[...].reshape(own0.shape)], axis=1
    )
    coulomb = jnp.dot(own_t[...], partner, preferred_element_type=jnp.float32)
    shift = energy_ref[4] + energy_ref[s]
    denominator = shift - row_ref[...] - col_ref[...]
    amplitude = ((2.0 * coulomb - coulomb.T) / denominator).astype(jnp.bfloat16)
    term = lax.dot_general(
        partner, amplitude, (((1,), (1,)), ((), ())), preferred_element_type=jnp.float32
    )

    @pl.when(s == 0)
    def _():
        total[...] = term

    @pl.when(s > 0)
    def _():
        total[...] += term

    @pl.when(s == pl.num_programs(0) - 1)
    def _():
        out_ref[...] = total[...].astype(out_ref.dtype)


def pair_terms(energies, owns, parts, virtual_energy):
    rows, half = owns[0].shape
    virt = 2 * half
    steps = parts[0].shape[1]
    whole = pl.BlockSpec((rows, half), lambda s: (0, 0))
    part = pl.BlockSpec((8, 1, rows // 8, half), lambda s: (0, s, 0, 0))
    smem = pl.BlockSpec(memory_space=pltpu.SMEM)
    return pl.pallas_call(
        pair_kernel,
        out_shape=jax.ShapeDtypeStruct((rows, virt), jnp.bfloat16),
        grid=(steps,),
        in_specs=[
            smem,
            whole,
            whole,
            part,
            part,
            pl.BlockSpec((virt, 1), lambda s: (0, 0)),
            pl.BlockSpec((1, virt), lambda s: (0, 0)),
        ],
        out_specs=pl.BlockSpec((rows, virt), lambda s: (0, 0)),
        scratch_shapes=[
            pltpu.VMEM((virt, rows), jnp.bfloat16),
            pltpu.VMEM((rows, virt), jnp.float32),
        ],
        compiler_params=pltpu.CompilerParams(vmem_limit_bytes=44 * 2**20),
        cost_estimate=pl.CostEstimate(
            flops=steps * 4 * rows * virt * virt,
            bytes_accessed=(steps + 2) * rows * virt * 2,
            transcendentals=0,
        ),
        name="pair_terms",
    )(energies, *owns, *parts, virtual_energy[:, None], virtual_energy[None, :])


def body(integrals, metric, occupied_energy, virtual_energy, plan):
    aux_rows = metric.shape[0]
    shard, _, virt = integrals.shape
    width = virt // CHUNKS
    y, x, yl, z, c = (lax.axis_index(name) for name, _ in SPLIT)
    place = (yl * 8 + z) * 2 + y
    wanted = lax.dynamic_index_in_dim(plan, place, 1, keepdims=False)
    own_energy = lax.dynamic_slice_in_dim(occupied_energy, (c * 4 + x) * 32 + place, 1)
    partner_energy = occupied_energy[wanted * 32 + place]
    energies = jnp.concatenate([partner_energy, own_energy])
    sent = integrals.reshape(shard, 16, 2, CHUNKS, width).transpose(3, 2, 1, 0, 4)
    owns, parts = [], []
    for k in range(CHUNKS):
        turned = lax.all_to_all(sent[k], "yh", 0, 0, tiled=True)
        turned = turned.transpose(1, 0, 2, 3).reshape(32, shard, width)
        received = lax.all_to_all(turned, AUX, 0, 0, tiled=True).reshape(aux_rows, width)
        own = jnp.dot(metric, received, preferred_element_type=jnp.float32).astype(jnp.bfloat16)
        owns.append(own)
        slices = lax.all_to_all(
            own.reshape(8, aux_rows // 8, width), PLACE, 0, 0, tiled=True
        )
        picked = jnp.stack(
            [
                lax.dynamic_index_in_dim(slices, wanted[s], 0, keepdims=False)
                for s in range(plan.shape[0])
            ]
        )
        along = lax.all_to_all(jnp.broadcast_to(picked, (4, *picked.shape)), "x", 0, 0, tiled=True)
        along = along.reshape(4, *picked.shape)
        both = lax.all_to_all(jnp.broadcast_to(along, (2, *along.shape)), "c", 0, 0, tiled=True)
        parts.append(both.reshape(8, *picked.shape))
    density = pair_terms(energies, owns, parts, virtual_energy)
    density = density.reshape(32, 2, shard // 2, virt)
    outs = []
    for k in range(2):
        gone = lax.all_to_all(density[:, k], AUX, 0, 0, tiled=True)
        gone = gone.reshape(16, 2, shard // 2, virt).transpose(1, 0, 2, 3)
        back = lax.all_to_all(gone, "yh", 0, 0, tiled=True)
        outs.append(back.transpose(2, 1, 0, 3).reshape(shard // 2, 32, virt))
    return jnp.concatenate(outs)


def solution(mesh):
    names = tuple(name for name, _ in SPLIT)
    split = Mesh(mesh.devices.reshape(*(size for _, size in SPLIT)), names)
    placed = P(AUX, ("yh", "x"), None)
    return jax.shard_map(
        body, mesh=split, in_specs=(placed, P(), P(), P(), P()), out_specs=placed, check_vma=False
    )
```

time: 370 us -> 357 us (0.965)
  blocking collectives: 123 us -> 48.8 us
  starting transfers between devices: 0.01 us -> 47.3 us
  waiting for transfers between devices: 170 us -> 195 us
  between operations: 28.6 us -> 7.96 us
  matrix products: 33.4 us -> 13.5 us
  Pallas kernels: 0 us -> 14.8 us
  local copies, waits for them, and re-layouts: 14 us -> 26.8 us
    all_to_all x0 -> x11, waiting for transfers between devices: none -> 195 us  [the longest x2 51.5 us: body(): lax.all_to_all(jnp.broadcast_to(picked, (4, *picked.shape)), 'x', 0, 0, t...]
    all_gather x1 -> x0, waiting for transfers between devices: 170 us -> none  [broadcast(): lax.all_gather(array, axis)]
    all_to_all x3, blocking collectives: 123 us -> 48.8 us  [the longest x1 32.2 us: body(): gone = lax.all_to_all(density[:, k], AUX, 0, 0, tiled=True)]
    all_to_all x0 -> x11, starting transfers between devices: none -> 47.3 us  [the longest x2 13.1 us: body(): lax.all_to_all(turned, AUX, 0, 0, tiled=True).reshape(aux_rows, width)]
    dot_general x9 -> x2, matrix products: 33.4 us -> 13.5 us  [body(): jnp.dot(metric, received, preferred_element_type=jnp.float32)]
    pallas_call x0 -> x1, Pallas kernels: none -> 14.8 us  [pair_terms(): pl.pallas_call(pair_kernel, out_shape=jax.ShapeDtypeStruct((rows, virt),...]
    slice x1 -> x4, local copies, waits for them, and re-layouts: 0.01 us -> 8.61 us  [the longest x3 8 us: body(): turned = lax.all_to_all(sent[k], 'yh', 0, 0, tiled=True)]
    dot_general x4 -> x0, local copies, waits for them, and re-layouts: 5.68 us -> none  [pair_term(): jnp.einsum('qia,qjb->ijab', own_block, partner, preferred_element_type=jn...]
  transfers between devices with their start and end apart: 1 -> 11, of which waited for: 1 -> 11; matrix products, arithmetic and copies ran while one was open for 1% -> 7% of each run, Pallas kernels for 0% -> 0%
where the time goes in v1:
time: 357 us; the launch traced here: 356 us
  waiting for transfers between devices  195 us (55%)
  blocking collectives  48.8 us (14%)
  starting transfers between devices  47.3 us (13%)
  local copies, waits for them, and re-layouts  26.8 us (8%)
  Pallas kernels  14.8 us (4%)
  matrix products  13.5 us (4%)
  between operations  7.96 us (2%)
    all_to_all x2, waiting for transfers between devices, body(): lax.all_to_all(jnp.broadcast_to(picked, (4, *picked.shape)), 'x', 0, 0, t...  51.5 us
    all_to_all x2, waiting for transfers between devices, body(): lax.all_to_all(turned, AUX, 0, 0, tiled=True).reshape(aux_rows, width)  49.9 us
    all_to_all x1, blocking collectives, body(): gone = lax.all_to_all(density[:, k], AUX, 0, 0, tiled=True)  32.2 us
    all_to_all x1, waiting for transfers between devices, body(): gone = lax.all_to_all(density[:, k], AUX, 0, 0, tiled=True)  27.1 us
    all_to_all x2, waiting for transfers between devices, body(): turned = lax.all_to_all(sent[k], 'yh', 0, 0, tiled=True)  26.2 us
    all_to_all x2, waiting for transfers between devices, body(): back = lax.all_to_all(gone, 'yh', 0, 0, tiled=True)  25.4 us
    all_to_all x2, blocking collectives, body(): lax.all_to_all(jnp.broadcast_to(along, (2, *along.shape)), 'c', 0, 0, til...  16.6 us
    all_to_all x2, waiting for transfers between devices, body(): lax.all_to_all(own.reshape(8, aux_rows // 8, width), PLACE, 0, 0, tiled=T...  15.1 us
  transfers between devices with their start and end apart: 11, of which 11 were waited for; matrix products, arithmetic and copies ran while one was open for 7% of the time, Pallas kernels for 0%

profile of v1, /device:TPU:32, one launch (start us, length us, event | category | flops | bytes accessed | tf_op | source)
XLA Modules:
  0.0 355.5 jit_solution(9537767175075969083)
XLA Ops:
  0.0 2.5 reshape.50
  2.6 3.8 %fusion.1 = (bf16[1,2,16,64,256]{4,0,1,2,3:T(2,128)(2,1)S(1)}, bf16[1,2,16,64,256]{4,0,1,2,3:T(2,128)(2,1)}) fusion(bf16[2,2,16,64,256]{4,0,1,2,3:T(2,128)(2,1)S(1)} %bitcast.52), kind=kLoop, calls=%fused_computation.23 | loop fusion | bytes 4194304 | tf_op jit(solution)/shard_map/slice | solution.py:96
  6.4 0.0 copy-start.3
  6.4 2.1 copy.39
  8.5 4.5 %all-to-all-start.2 = ((bf16[2,16,64,256]{3,2,1,0:T(8,128)(2,1)}), bf16[2,16,64,256]{3,2,1,0:T(8,128)(2,1)S(1)}, u32[]{:S(2)}, u32[]{:S(2)}) async-start(bf16[2,16,64,256]{3,2,1,0:T(8,128)(2,1)} %bitcast.46), calls=%async_computation.2 | async-start | bytes 2097152 | tf_op jit(solution)/shard_map/all_to_all | solution.py:96
  12.9 0.0 copy-done.3
  12.9 2.1 copy.40
  15.0 13.0 %all-to-all-done.2 = bf16[2,16,64,256]{3,2,1,0:T(8,128)(2,1)S(1)} async-done(((bf16[2,16,64,256]{3,2,1,0:T(8,128)(2,1)}), bf16[2,16,64,256]{3,2,1,0:T(8,128)(2,1)S(1)}, u32[]{:S(2)}, u32[]{:S(2)}) %all-to-all-start.2) | async-done | bytes 1048608 | tf_op jit(solution)/shard_map/all_to_all | solution.py:96
  28.0 3.6 %all-to-all-start = ((bf16[2,16,64,256]{3,2,1,0:T(8,128)(2,1)}), bf16[2,16,64,256]{3,2,1,0:T(8,128)(2,1)S(1)}, u32[]{:S(2)}, u32[]{:S(2)}) async-start(bf16[2,16,64,256]{3,2,1,0:T(8,128)(2,1)} %bitcast.47), calls=%async_computation | async-start | bytes 2097152 | tf_op jit(solution)/shard_map/all_to_all | solution.py:96
  31.6 1.1 copy.26
  32.7 13.2 %all-to-all-done = bf16[2,16,64,256]{3,2,1,0:T(8,128)(2,1)S(1)} async-done(((bf16[2,16,64,256]{3,2,1,0:T(8,128)(2,1)}), bf16[2,16,64,256]{3,2,1,0:T(8,128)(2,1)S(1)}, u32[]{:S(2)}, u32[]{:S(2)}) %all-to-all-start) | async-done | bytes 1048608 | tf_op jit(solution)/shard_map/all_to_all | solution.py:96
  45.8 9.4 %all-to-all-start.3 = ((bf16[32,64,256]{2,1,0:T(8,128)(2,1)}), bf16[32,64,256]{2,1,0:T(8,128)(2,1)S(1)}, u32[]{:S(2)}, u32[]{:S(2)}) async-start(bf16[32,64,256]{2,1,0:T(8,128)(2,1)} %bitcast.7), calls=%async_computation.3 | async-start | bytes 2097152 | tf_op jit(solution)/shard_map/all_to_all | solution.py:98
  55.3 1.0 copy.24
  56.3 27.9 %all-to-all-done.3 = bf16[32,64,256]{2,1,0:T(8,128)(2,1)S(1)} async-done(((bf16[32,64,256]{2,1,0:T(8,128)(2,1)}), bf16[32,64,256]{2,1,0:T(8,128)(2,1)S(1)}, u32[]{:S(2)}, u32[]{:S(2)}) %all-to-all-start.3) | async-done | bytes 1048608 | tf_op jit(solution)/shard_map/all_to_all | solution.py:98
  84.2 3.7 %all-to-all-start.1 = ((bf16[32,64,256]{2,1,0:T(8,128)(2,1)}), bf16[32,64,256]{2,1,0:T(8,128)(2,1)S(1)}, u32[]{:S(2)}, u32[]{:S(2)}) async-start(bf16[32,64,256]{2,1,0:T(8,128)(2,1)} %bitcast.3), calls=%async_computation.1 | async-start | bytes 2097152 | tf_op jit(solution)/shard_map/all_to_all | solution.py:98
  87.9 6.7 %convolution_convert_fusion.own1 = bf16[2048,256]{1,0:T(8,128)(2,1)} fusion(bf16[2048,2048]{1,0:T(8,128)(2,1)} %param.6, bf16[2048,256]{1,0:T(8,128)(2,1)S(1)} %bitcast.60), kind=kOutput, calls=%fused_computation.1 | convolution fusion | flops 2148007936 | bytes 10485760 | tf_op jit(solution)/shard_map/dot_general | solution.py:99
  94.7 22.0 %all-to-all-done.1 = bf16[32,64,256]{2,1,0:T(8,128)(2,1)S(1)} async-done(((bf16[32,64,256]{2,1,0:T(8,128)(2,1)}), bf16[32,64,256]{2,1,0:T(8,128)(2,1)S(1)}, u32[]{:S(2)}, u32[]{:S(2)}) %all-to-all-start.1) | async-done | bytes 1048608 | tf_op jit(solution)/shard_map/all_to_all | solution.py:98
  116.7 4.3 %all-to-all-start.7 = ((bf16[8,256,256]{2,1,0:T(8,128)(2,1)}), bf16[8,256,256]{2,1,0:T(8,128)(2,1)S(1)}, u32[]{:S(2)}, u32[]{:S(2)}) async-start(bf16[8,256,256]{2,1,0:T(8,128)(2,1)} %bitcast.15), calls=%async_computation.7 | async-start | bytes 2097152 | tf_op jit(solution)/shard_map/all_to_all | solution.py:101
  121.0 6.8 %convolution_convert_fusion.1.own0 = bf16[2048,256]{1,0:T(8,128)(2,1)} fusion(bf16[2048,2048]{1,0:T(8,128)(2,1)} %param.6, bf16[2048,256]{1,0:T(8,128)(2,1)S(1)} %bitcast.61), kind=kOutput, calls=%fused_computation.2 | convolution fusion | flops 2148007936 | bytes 10485760 | tf_op jit(solution)/shard_map/dot_general | solution.py:99
  127.7 0.0 copy-start.4
  127.7 8.5 %all-to-all-done.7 = bf16[8,256,256]{2,1,0:T(8,128)(2,1)S(1)} async-done(((bf16[8,256,256]{2,1,0:T(8,128)(2,1)}), bf16[8,256,256]{2,1,0:T(8,128)(2,1)S(1)}, u32[]{:S(2)}, u32[]{:S(2)}) %all-to-all-start.7) | async-done | bytes 1048608 | tf_op jit(solution)/shard_map/all_to_all | solution.py:101
  136.2 3.6 %all-to-all-start.4 = ((bf16[8,256,256]{2,1,0:T(8,128)(2,1)}), bf16[8,256,256]{2,1,0:T(8,128)(2,1)S(1)}, u32[]{:S(2)}, u32[]{:S(2)}) async-start(bf16[8,256,256]{2,1,0:T(8,128)(2,1)} %bitcast.9), calls=%async_computation.4 | async-start | bytes 2097152 | tf_op jit(solution)/shard_map/all_to_all | solution.py:101
  139.8 0.0 copy-done.4
  139.8 0.2 fusion
  140.0 0.6 fusion.2
  148.3 6.6 %all-to-all-done.4 = bf16[8,256,256]{2,1,0:T(8,128)(2,1)S(1)} async-done(((bf16[8,256,256]{2,1,0:T(8,128)(2,1)}), bf16[8,256,256]{2,1,0:T(8,128)(2,1)S(1)}, u32[]{:S(2)}, u32[]{:S(2)}) %all-to-all-start.4) | async-done | bytes 1048608 | tf_op jit(solution)/shard_map/all_to_all | solution.py:101
  155.0 0.1 constant_dynamic-slice_fusion.3
  155.0 0.1 pad_maximum_fusion.1
  155.1 1.5 broadcast_in_dim.19
  156.6 3.6 %all-to-all-start.5 = ((bf16[4,4,256,256]{3,2,1,0:T(8,128)(2,1)}), bf16[4,4,256,256]{3,2,1,0:T(8,128)(2,1)S(1)}, u32[]{:S(2)}, u32[]{:S(2)}) async-start(bf16[4,4,256,256]{3,2,1,0:T(8,128)(2,1)} %broadcast_in_dim.19), calls=%async_computation.5 | async-start | bytes 4194304 | tf_op jit(solution)/shard_map/all_to_all | solution.py:110
  160.3 0.1 pad_maximum_fusion.2
  160.3 26.9 %all-to-all-done.5 = bf16[4,4,256,256]{3,2,1,0:T(8,128)(2,1)S(1)} async-done(((bf16[4,4,256,256]{3,2,1,0:T(8,128)(2,1)}), bf16[4,4,256,256]{3,2,1,0:T(8,128)(2,1)S(1)}, u32[]{:S(2)}, u32[]{:S(2)}) %all-to-all-start.5) | async-done | bytes 2097184 | tf_op jit(solution)/shard_map/all_to_all | solution.py:110
  187.2 0.5 broadcast_in_dim.20
  187.7 8.2 %all_to_all.70 = bf16[2,4,4,256,256]{4,3,2,1,0:T(8,128)(2,1)} all-to-all(bf16[2,4,4,256,256]{4,3,2,1,0:T(8,128)(2,1)S(1)} %broadcast_in_dim.20), channel_id=1, replica_groups=mesh['yh'=2,'x'=4,'yl'=2,'z'=8,'c'=2] {'c'}, dimensions={0} | all-to-all | bytes 8388608 | tf_op jit(solution)/shard_map/all_to_all | solution.py:112
  195.8 1.5 broadcast_in_dim.21
  197.4 0.0 copy-start.2
  197.4 0.0 copy-start.1
  197.4 3.7 %all-to-all-start.8 = ((bf16[4,4,256,256]{3,2,1,0:T(8,128)(2,1)}), bf16[4,4,256,256]{3,2,1,0:T(8,128)(2,1)S(1)}, u32[]{:S(2)}, u32[]{:S(2)}) async-start(bf16[4,4,256,256]{3,2,1,0:T(8,128)(2,1)} %broadcast_in_dim.21), calls=%async_computation.8 | async-start | bytes 4194304 | tf_op jit(solution)/shard_map/all_to_all | solution.py:110
  201.1 0.0 copy-done.2
  201.1 0.7 dynamic_slice.33
  201.8 0.6 gather_fusion
  202.4 0.0 copy-done.1
  202.4 0.1 copy.27.row_ref
  202.6 0.8 pad_maximum_fusion.3.energy_ref
  203.4 24.6 %all-to-all-done.8 = bf16[4,4,256,256]{3,2,1,0:T(8,128)(2,1)S(1)} async-done(((bf16[4,4,256,256]{3,2,1,0:T(8,128)(2,1)}), bf16[4,4,256,256]{3,2,1,0:T(8,128)(2,1)S(1)}, u32[]{:S(2)}, u32[]{:S(2)}) %all-to-all-start.8) | async-done | bytes 2097184 | tf_op jit(solution)/shard_map/all_to_all | solution.py:110
  228.0 0.5 broadcast_in_dim.22
  228.5 0.0 copy-start
  228.5 8.5 %all_to_all.71 = bf16[2,4,4,256,256]{4,3,2,1,0:T(8,128)(2,1)} all-to-all(bf16[2,4,4,256,256]{4,3,2,1,0:T(8,128)(2,1)S(1)} %broadcast_in_dim.22), channel_id=1, replica_groups=mesh['yh'=2,'x'=4,'yl'=2,'z'=8,'c'=2] {'c'}, dimensions={0} | all-to-all | bytes 8388608 | tf_op jit(solution)/shard_map/all_to_all | solution.py:112
  236.9 0.0 copy-done
  236.9 14.8 %pair_terms.1 = bf16[2048,512]{1,0:T(8,128)(2,1)S(1)} custom-call(f32[5]{0:T(128)S(1)} %pad_maximum_fusion.3.energy_ref, bf16[2048,256]{1,0:T(8,128)(2,1)} %convolution_convert_fusion.1.own0, bf16[2048,256]{1,0:T(8,128)(2,1)} %convolution_convert_fusion.own1, bf16[8,4,256,256]{3,2,1,0:T(8,128)(2,1)S(1)} %bitcast.48, bf16[8,4,256,256]{3,2,1,0:T(8,128)(2,1)} %bitcast.53, ...), custom_call_target="tpu_custom_call" | custom-call | flops 8589934592 | bytes 12582912 | tf_op jit(solution)/shard_map/pair_terms/pallas_call | solution.py:55
  251.7 1.2 slice_bitcast_fusion.1
  253.0 32.2 %all_to_all.72 = bf16[32,32,512]{2,1,0:T(8,128)(2,1)S(1)} all-to-all(bf16[32,32,512]{2,1,0:T(8,128)(2,1)S(1)} %get-tuple-element.8), channel_id=1, replica_groups=mesh['yh'=2,'x'=4,'yl'=2,'z'=8,'c'=2] {'yl','z','c'}, dimensions={0} | all-to-all | bytes 2097152 | tf_op jit(solution)/shard_map/all_to_all | solution.py:118
  285.2 3.7 %all-to-all-start.10 = ((bf16[32,32,512]{2,1,0:T(8,128)(2,1)}), bf16[32,32,512]{2,1,0:T(8,128)(2,1)S(1)}, u32[]{:S(2)}, u32[]{:S(2)}) async-start(bf16[32,32,512]{2,1,0:T(8,128)(2,1)} %get-tuple-element.7), calls=%async_computation.10 | async-start | bytes 2097152 | tf_op jit(solution)/shard_map/all_to_all | solution.py:118
  288.9 1.6 copy.32
  290.5 27.1 %all-to-all-done.10 = bf16[32,32,512]{2,1,0:T(8,128)(2,1)S(1)} async-done(((bf16[32,32,512]{2,1,0:T(8,128)(2,1)}), bf16[32,32,512]{2,1,0:T(8,128)(2,1)S(1)}, u32[]{:S(2)}, u32[]{:S(2)}) %all-to-all-start.10) | async-done | bytes 1048608 | tf_op jit(solution)/shard_map/all_to_all | solution.py:118
  317.6 3.6 %all-to-all-start.13 = ((bf16[2,16,32,512]{3,1,2,0:T(8,128)(2,1)}), bf16[2,16,32,512]{3,1,2,0:T(8,128)(2,1)S(1)}, u32[]{:S(2)}, u32[]{:S(2)}) async-start(bf16[2,16,32,512]{3,1,2,0:T(8,128)(2,1)} %copy.32), calls=%async_computation.13 | async-start | bytes 2097152 | tf_op jit(solution)/shard_map/all_to_all | solution.py:120
  321.2 1.6 copy.29
  322.7 12.6 %all-to-all-done.13 = bf16[2,16,32,512]{3,1,2,0:T(8,128)(2,1)S(1)} async-done(((bf16[2,16,32,512]{3,1,2,0:T(8,128)(2,1)}), bf16[2,16,32,512]{3,1,2,0:T(8,128)(2,1)S(1)}, u32[]{:S(2)}, u32[]{:S(2)}) %all-to-all-start.13) | async-done | bytes 1048608 | tf_op jit(solution)/shard_map/all_to_all | solution.py:120
  335.4 3.6 %all-to-all-start.11 = ((bf16[2,16,32,512]{3,1,2,0:T(8,128)(2,1)}), bf16[2,16,32,512]{3,1,2,0:T(8,128)(2,1)S(1)}, u32[]{:S(2)}, u32[]{:S(2)}) async-start(bf16[2,16,32,512]{3,1,2,0:T(8,128)(2,1)} %copy.29), calls=%async_computation.11 | async-start | bytes 2097152 | tf_op jit(solution)/shard_map/all_to_all | solution.py:120
  339.0 0.6 copy.33
  339.6 12.7 %all-to-all-done.11 = bf16[2,16,32,512]{3,1,2,0:T(8,128)(2,1)S(1)} async-done(((bf16[2,16,32,512]{3,1,2,0:T(8,128)(2,1)}), bf16[2,16,32,512]{3,1,2,0:T(8,128)(2,1)S(1)}, u32[]{:S(2)}, u32[]{:S(2)}) %all-to-all-start.11) | async-done | bytes 1048608 | tf_op jit(solution)/shard_map/all_to_all | solution.py:120
  352.3 0.6 copy.30
  352.9 0.1 pad_maximum_fusion
  353.0 2.5 copy.34
  (1 shorter events, 0.0 us)
Async XLA Ops:
  6.4 6.6 %copy-start.3 = (bf16[1,2,16,64,256]{4,0,1,2,3:T(2,128)(2,1)S(1)}, bf16[1,2,16,64,256]{4,0,1,2,3:T(2,128)(2,1)}, u32[]{:S(2)}) copy-start(bf16[1,2,16,64,256]{4,0,1,2,3:T(2,128)(2,1)} %get-tuple-element.10) | copy-start | bytes 3145732
  8.5 19.6 %all-to-all-start.2 = ((bf16[2,16,64,256]{3,2,1,0:T(8,128)(2,1)}), bf16[2,16,64,256]{3,2,1,0:T(8,128)(2,1)S(1)}, u32[]{:S(2)}, u32[]{:S(2)}) async-start(bf16[2,16,64,256]{3,2,1,0:T(8,128)(2,1)} %bitcast.46), calls=%async_computation.2 | async-start | bytes 2097152 | tf_op jit(solution)/shard_map/all_to_all | solution.py:96
  28.0 17.8 %all-to-all-start = ((bf16[2,16,64,256]{3,2,1,0:T(8,128)(2,1)}), bf16[2,16,64,256]{3,2,1,0:T(8,128)(2,1)S(1)}, u32[]{:S(2)}, u32[]{:S(2)}) async-start(bf16[2,16,64,256]{3,2,1,0:T(8,128)(2,1)} %bitcast.47), calls=%async_computation | async-start | bytes 2097152 | tf_op jit(solution)/shard_map/all_to_all | solution.py:96
  45.8 38.4 %all-to-all-start.3 = ((bf16[32,64,256]{2,1,0:T(8,128)(2,1)}), bf16[32,64,256]{2,1,0:T(8,128)(2,1)S(1)}, u32[]{:S(2)}, u32[]{:S(2)}) async-start(bf16[32,64,256]{2,1,0:T(8,128)(2,1)} %bitcast.7), calls=%async_computation.3 | async-start | bytes 2097152 | tf_op jit(solution)/shard_map/all_to_all | solution.py:98
  84.2 32.4 %all-to-all-start.1 = ((bf16[32,64,256]{2,1,0:T(8,128)(2,1)}), bf16[32,64,256]{2,1,0:T(8,128)(2,1)S(1)}, u32[]{:S(2)}, u32[]{:S(2)}) async-start(bf16[32,64,256]{2,1,0:T(8,128)(2,1)} %bitcast.3), calls=%async_computation.1 | async-start | bytes 2097152 | tf_op jit(solution)/shard_map/all_to_all | solution.py:98
  116.7 19.5 %all-to-all-start.7 = ((bf16[8,256,256]{2,1,0:T(8,128)(2,1)}), bf16[8,256,256]{2,1,0:T(8,128)(2,1)S(1)}, u32[]{:S(2)}, u32[]{:S(2)}) async-start(bf16[8,256,256]{2,1,0:T(8,128)(2,1)} %bitcast.15), calls=%async_computation.7 | async-start | bytes 2097152 | tf_op jit(solution)/shard_map/all_to_all | solution.py:101
  127.7 12.0 %copy-start.4 = (s32[4,32]{1,0:T(4,128)S(1)}, s32[4,32]{1,0:T(4,128)}, u32[]{:S(2)}) copy-start(s32[4,32]{1,0:T(4,128)} %param.9) | copy-start | bytes 1540
  136.2 18.8 %all-to-all-start.4 = ((bf16[8,256,256]{2,1,0:T(8,128)(2,1)}), bf16[8,256,256]{2,1,0:T(8,128)(2,1)S(1)}, u32[]{:S(2)}, u32[]{:S(2)}) async-start(bf16[8,256,256]{2,1,0:T(8,128)(2,1)} %bitcast.9), calls=%async_computation.4 | async-start | bytes 2097152 | tf_op jit(solution)/shard_map/all_to_all | solution.py:101
  156.6 30.6 %all-to-all-start.5 = ((bf16[4,4,256,256]{3,2,1,0:T(8,128)(2,1)}), bf16[4,4,256,256]{3,2,1,0:T(8,128)(2,1)S(1)}, u32[]{:S(2)}, u32[]{:S(2)}) async-start(bf16[4,4,256,256]{3,2,1,0:T(8,128)(2,1)} %broadcast_in_dim.19), calls=%async_computation.5 | async-start | bytes 4194304 | tf_op jit(solution)/shard_map/all_to_all | solution.py:110
  197.4 3.8 %copy-start.2 = (f32[256]{0:T(256)S(1)}, f32[256]{0:T(256)}, u32[]{:S(2)}) copy-start(f32[256]{0:T(256)} %param.7) | copy-start | bytes 3076
  197.4 5.1 %copy-start.1 = (f32[512]{0:T(512)S(1)}, f32[512]{0:T(512)}, u32[]{:S(2)}) copy-start(f32[512]{0:T(512)} %param.8) | copy-start | bytes 6148
  197.4 30.6 %all-to-all-start.8 = ((bf16[4,4,256,256]{3,2,1,0:T(8,128)(2,1)}), bf16[4,4,256,256]{3,2,1,0:T(8,128)(2,1)S(1)}, u32[]{:S(2)}, u32[]{:S(2)}) async-start(bf16[4,4,256,256]{3,2,1,0:T(8,128)(2,1)} %broadcast_in_dim.21), calls=%async_computation.8 | async-start | bytes 4194304 | tf_op jit(solution)/shard_map/all_to_all | solution.py:110
  228.5 8.5 %copy-start = (bf16[2,4,4,256,256]{4,3,2,1,0:T(8,128)(2,1)S(1)}, bf16[2,4,4,256,256]{4,3,2,1,0:T(8,128)(2,1)}, u32[]{:S(2)}) copy-start(bf16[2,4,4,256,256]{4,3,2,1,0:T(8,128)(2,1)} %all_to_all.70) | copy-start | bytes 12582916
  285.2 32.4 %all-to-all-start.10 = ((bf16[32,32,512]{2,1,0:T(8,128)(2,1)}), bf16[32,32,512]{2,1,0:T(8,128)(2,1)S(1)}, u32[]{:S(2)}, u32[]{:S(2)}) async-start(bf16[32,32,512]{2,1,0:T(8,128)(2,1)} %get-tuple-element.7), calls=%async_computation.10 | async-start | bytes 2097152 | tf_op jit(solution)/shard_map/all_to_all | solution.py:118
  317.6 17.8 %all-to-all-start.13 = ((bf16[2,16,32,512]{3,1,2,0:T(8,128)(2,1)}), bf16[2,16,32,512]{3,1,2,0:T(8,128)(2,1)S(1)}, u32[]{:S(2)}, u32[]{:S(2)}) async-start(bf16[2,16,32,512]{3,1,2,0:T(8,128)(2,1)} %copy.32), calls=%async_computation.13 | async-start | bytes 2097152 | tf_op jit(solution)/shard_map/all_to_all | solution.py:120
  335.4 16.9 %all-to-all-start.11 = ((bf16[2,16,32,512]{3,1,2,0:T(8,128)(2,1)}), bf16[2,16,32,512]{3,1,2,0:T(8,128)(2,1)S(1)}, u32[]{:S(2)}, u32[]{:S(2)}) async-start(bf16[2,16,32,512]{3,1,2,0:T(8,128)(2,1)} %copy.29), calls=%async_computation.11 | async-start | bytes 2097152 | tf_op jit(solution)/shard_map/all_to_all | solution.py:120
